TPU v7x, 256 devices: a whole 4x4x8 slice. The times are simulated.
256 devices in a mesh: dp: 16 (over y, z_hi, core), mp: 16 (over x, z_lo).
Axes of the slice: x: 4, y: 4, z: 8 (z_hi: 2, z_lo: 4; z = z_hi * 4 + z_lo), core: 2. Of those that a mesh axis runs over, the one named last changes fastest.
Arguments:
- skip_stream_arriving: float32 [4096, 2304], P('dp', 'mp'), may hold values from -170 to 170
- chosen_specialists: int32 [4096, 2], P('dp'), may hold values from 0 to 3, all different within a row; in each aligned block of 256 rows (0 to 255, 256 to 511, ...) at most 160 rows name the same one
- sequence_piece_tallies: int32 [16, 4], P('dp'), may hold values from 1 to 128, 256 in all within a row
- premix_rmsnorm_gain: float32 [2304], P('mp'), may hold values from 0.1 to 1.9
- dispatcher_weights: bfloat16 [2304, 4], replicated, may hold values from -0.125 to 0.125
- specialist_switch_weights: bfloat16 [4, 2304, 5760], P(None, 'dp', 'mp'), may hold values from -0.125 to 0.125
- specialist_expand_weights: bfloat16 [4, 2304, 5760], P(None, 'dp', 'mp'), may hold values from -0.125 to 0.125
- specialist_contract_weights: bfloat16 [4, 5760, 2304], P(None, 'mp', 'dp'), may hold values from -0.109375 to 0.109375
- terminal_rmsnorm_gain: float32 [2304], replicated, may hold values from 0.1 to 1.9
- lexicon_projector_weights: bfloat16 [2304, 131072], P(None, ('dp', 'mp')), may hold values from -12 to 12
- softness_per_sequence: float32 [64], replicated, may hold values from 0.02 to 1.5
Outputs:
- new_hidden: float32 [4096, 2304], P('dp', 'mp')
- logprobs: float32 [64, 131072], P(None, ('dp', 'mp'))
Inputs may be any that keep to these rules, and one draw needn't show every extreme that they name: `chosen_specialists`: in the 256 rows of each data group no expert is named by more than 160 rows, a bound that some block reaches. `sequence_piece_tallies`: each row sums to 256; its largest entry is 128.
All inputs are finite; a program needn't handle non-finite values.
Results may differ from a plain program's by a relative error of at most 0.0014.
Values may be sent and summed in bfloat16 or wider, within the bound.
A program may use at most 128 MiB of HBM per device.

v0:
```python
import math
import jax
import jax.numpy as jnp
from jax import lax
from jax.sharding import PartitionSpec as P

EMBED_DIMENSION = 2304
CAP = 160
branch_scale = 1.4 / math.sqrt(40.0)
epsilon = 1e-05


def slot_tables(routes_grp, expert, capacity):
    count = routes_grp.shape[0]
    hit = jnp.any(routes_grp == expert, axis=1)
    second = (routes_grp[:, 1] == expert).astype(jnp.int32)
    order = jnp.cumsum(hit.astype(jnp.int32), dtype=jnp.int32) - 1
    target = jnp.where(hit, order, capacity)
    tokens = jnp.arange(count, dtype=jnp.int32)
    slot_rows = jnp.zeros((capacity,), jnp.int32).at[target].set(tokens, mode="drop")
    live = jnp.zeros((capacity,), jnp.float32).at[target].set(1.0, mode="drop")
    which = jnp.zeros((capacity,), jnp.int32).at[target].set(second, mode="drop")
    return (slot_rows, live, which)


def body(
    skip_stream_arriving,
    chosen_specialists,
    sequence_piece_tallies,
    premix_rmsnorm_gain,
    dispatcher_weights,
    specialist_switch_weights,
    specialist_expand_weights,
    specialist_contract_weights,
    terminal_rmsnorm_gain,
    lexicon_projector_weights,
    softness_per_sequence,
):
    tok_rows = skip_stream_arriving.shape[0]
    local_width = skip_stream_arriving.shape[1]
    experts = specialist_switch_weights.shape[0]
    unit_cols = specialist_switch_weights.shape[2]
    squares = lax.psum(jnp.sum(skip_stream_arriving * skip_stream_arriving, axis=1), "mp")
    normed_local = (
        skip_stream_arriving
        * lax.rsqrt(squares / EMBED_DIMENSION + epsilon)[:, None]
        * premix_rmsnorm_gain
    ).astype(jnp.bfloat16)
    features = lax.all_gather(normed_local, "mp", axis=1, tiled=True)
    router = jnp.dot(features, dispatcher_weights, preferred_element_type=jnp.float32)
    mixing = jax.nn.softmax(jnp.take_along_axis(router, chosen_specialists, axis=1), axis=1)
    tables = [slot_tables(chosen_specialists, expert, CAP) for expert in range(experts)]
    inputs = jnp.stack([features[table[0]] for table in tables])
    scales = jnp.stack([mixing[table[0], table[2]] * table[1] for table in tables])
    pieces_out = []
    for expert in range(experts):
        rows_in = inputs[expert]

        def add_pair(carry, pieces, start, rows_in=rows_in):
            return (
                jnp.dot(rows_in, pieces[0], preferred_element_type=jnp.float32),
                jnp.dot(rows_in, pieces[1], preferred_element_type=jnp.float32),
            )

        empty = jnp.zeros((CAP, unit_cols), jnp.float32)
        gate, up_part = add_pair(
            (empty, empty),
            (
                lax.all_gather(specialist_switch_weights[expert], "dp", axis=0, tiled=True),
                lax.all_gather(specialist_expand_weights[expert], "dp", axis=0, tiled=True),
            ),
            jnp.int32(0),
        )
        act = (jax.nn.silu(gate) * up_part).astype(jnp.bfloat16)

        def project(piece, start, act=act):
            return jnp.dot(act, piece, preferred_element_type=jnp.float32)

        pieces_out.append(
            project(
                lax.all_gather(specialist_contract_weights[expert], "dp", axis=1, tiled=True),
                jnp.int32(0),
            )
        )
    outputs = jnp.stack(pieces_out)
    combined = jnp.zeros((tok_rows, EMBED_DIMENSION), jnp.float32)
    for expert in range(experts):
        combined = combined.at[tables[expert][0]].add(outputs[expert] * scales[expert][:, None])
    branch = lax.psum_scatter(
        combined.astype(jnp.bfloat16), "mp", scatter_dimension=1, tiled=True
    ).astype(jnp.float32)
    new_hidden = skip_stream_arriving + branch_scale * branch
    ends_index = jnp.cumsum(sequence_piece_tallies[0], dtype=jnp.int32) - 1
    end_local = new_hidden[ends_index]
    groups = lax.axis_size("dp")
    columns_count = lax.axis_size("mp")
    req_count = ends_index.shape[0]
    end_squares = lax.psum(jnp.sum(end_local * end_local, axis=1), "mp")
    gain_local = lax.dynamic_slice_in_dim(
        terminal_rmsnorm_gain, lax.axis_index("mp") * local_width, local_width
    )
    end_normed = (
        end_local * lax.rsqrt(end_squares / EMBED_DIMENSION + epsilon)[:, None] * gain_local
    ).astype(jnp.bfloat16)
    shaped = lax.all_gather(end_normed[None], ("dp", "mp"), axis=0, tiled=True).reshape(
        groups, columns_count, req_count, local_width
    )
    lexicon_projector_feed = shaped.transpose(0, 2, 1, 3).reshape(
        groups * req_count, columns_count * local_width
    )
    lexicon_logit_values = jnp.dot(
        lexicon_projector_feed, lexicon_projector_weights, preferred_element_type=jnp.float32
    ) / (EMBED_DIMENSION / 256.0 * softness_per_sequence[:, None])
    largest = lax.pmax(jnp.max(lexicon_logit_values, axis=1), ("dp", "mp"))
    total_exp = lax.psum(
        jnp.sum(jnp.exp(lexicon_logit_values - largest[:, None]), axis=1), ("dp", "mp")
    )
    logprobs = lexicon_logit_values - largest[:, None] - jnp.log(total_exp)[:, None]
    return (new_hidden, logprobs)


def solution(mesh):
    return jax.shard_map(
        body,
        mesh=mesh,
        in_specs=(
            P("dp", "mp"),
            P("dp", None),
            P("dp", None),
            P("mp"),
            P(),
            P(None, "dp", "mp"),
            P(None, "dp", "mp"),
            P(None, "mp", "dp"),
            P(),
            P(None, ("dp", "mp")),
            P(),
        ),
        out_specs=(P("dp", "mp"), P(None, ("dp", "mp"))),
        check_vma=False,
    )
```

profile of v0, /device:TPU:1, one launch (start us, length us, event | category | flops | bytes accessed | tf_op | source)
XLA Modules:
  0.0 1764.0 jit_solution(12189918322459456357)
XLA Ops:
  8.4 38.4 %psum.21 = f32[256]{0:T(256)S(1)} all-reduce(f32[256]{0:T(256)S(1)} %multiply_reduce_fusion), channel_id=1, replica_groups=mesh['dp'=16,'mp'=16] {'mp'}, use_global_device_ids=true, to_apply=%region_5.6 | all-reduce | flops 256 | bytes 2048 | tf_op jit(solution)/shard_map/psum | solution.py:43
  84.2 43.0 %all-gather.26.cloned.1.call-done = bf16[256,2304]{0,1:T(8,128)(2,1)} async-done(((bf16[256,144]{0,1:T(8,128)(2,1)}), bf16[256,2304]{0,1:T(8,128)(2,1)}) %all-gather.26.cloned.1.call-update) | async-done | bytes 1179664 | tf_op jit(solution)/shard_map/all_gather | solution.py:49
  128.7 4.9 gather_fusion.9
  133.9 2.5 gather_fusion.3
  136.4 2.5 gather_fusion.1
  144.7 2.6 gather_fusion.5
  149.4 2.6 gather_fusion.7
  157.0 42.0 %all-gather.28.cloned.1.call-done = bf16[1,2304,360]{2,1,0:T(8,128)(2,1)} async-done(((bf16[1,144,360]{2,1,0:T(8,128)(2,1)}), bf16[1,2304,360]{2,1,0:T(8,128)(2,1)}) %all-gather.28.cloned.1.call-update) | async-done | bytes 1658896 | tf_op jit(solution)/shard_map/all_gather | solution.py:69
  201.2 56.7 %all-gather.30.cloned.1.call-done = bf16[1,2304,360]{2,1,0:T(8,128)(2,1)} async-done(((bf16[1,144,360]{2,1,0:T(8,128)(2,1)}), bf16[1,2304,360]{2,1,0:T(8,128)(2,1)}) %all-gather.30.cloned.1.call-update) | async-done | bytes 1658896 | tf_op jit(solution)/shard_map/all_gather | solution.py:70
  257.9 58.8 %all-gather.32.cloned.1.call-done = bf16[1,360,2304]{1,2,0:T(8,128)(2,1)} async-done(((bf16[1,360,144]{1,2,0:T(8,128)(2,1)}), bf16[1,360,2304]{1,2,0:T(8,128)(2,1)}) %all-gather.32.cloned.1.call-update) | async-done | bytes 1658896 | tf_op jit(solution)/shard_map/all_gather | solution.py:81
  316.8 4.4 convolution_multiply_fusion.3
  321.2 5.2 scatter_custom_fusion.3
  326.4 49.2 %all-gather.34.cloned.1.call-done = bf16[1,2304,360]{2,1,0:T(8,128)(2,1)} async-done(((bf16[1,144,360]{2,1,0:T(8,128)(2,1)}), bf16[1,2304,360]{2,1,0:T(8,128)(2,1)}) %all-gather.34.cloned.1.call-update) | async-done | bytes 1658896 | tf_op jit(solution)/shard_map/all_gather | solution.py:69
  377.6 56.8 %all-gather.36.cloned.1.call-done = bf16[1,2304,360]{2,1,0:T(8,128)(2,1)} async-done(((bf16[1,144,360]{2,1,0:T(8,128)(2,1)}), bf16[1,2304,360]{2,1,0:T(8,128)(2,1)}) %all-gather.36.cloned.1.call-update) | async-done | bytes 1658896 | tf_op jit(solution)/shard_map/all_gather | solution.py:70
  434.4 59.5 %all-gather.38.cloned.1.call-done = bf16[1,360,2304]{1,2,0:T(8,128)(2,1)} async-done(((bf16[1,360,144]{1,2,0:T(8,128)(2,1)}), bf16[1,360,2304]{1,2,0:T(8,128)(2,1)}) %all-gather.38.cloned.1.call-update) | async-done | bytes 1658896 | tf_op jit(solution)/shard_map/all_gather | solution.py:81
  494.0 4.4 convolution_multiply_fusion.2
  498.4 6.6 scatter_fusion
  504.9 48.0 %all-gather.40.cloned.1.call-done = bf16[1,2304,360]{2,1,0:T(8,128)(2,1)} async-done(((bf16[1,144,360]{2,1,0:T(8,128)(2,1)}), bf16[1,2304,360]{2,1,0:T(8,128)(2,1)}) %all-gather.40.cloned.1.call-update) | async-done | bytes 1658896 | tf_op jit(solution)/shard_map/all_gather | solution.py:69
  555.0 56.9 %all-gather.42.cloned.1.call-done = bf16[1,2304,360]{2,1,0:T(8,128)(2,1)} async-done(((bf16[1,144,360]{2,1,0:T(8,128)(2,1)}), bf16[1,2304,360]{2,1,0:T(8,128)(2,1)}) %all-gather.42.cloned.1.call-update) | async-done | bytes 1658896 | tf_op jit(solution)/shard_map/all_gather | solution.py:70
  611.9 58.8 %all-gather.44.cloned.1.call-done = bf16[1,360,2304]{1,2,0:T(8,128)(2,1)} async-done(((bf16[1,360,144]{1,2,0:T(8,128)(2,1)}), bf16[1,360,2304]{1,2,0:T(8,128)(2,1)}) %all-gather.44.cloned.1.call-update) | async-done | bytes 1658896 | tf_op jit(solution)/shard_map/all_gather | solution.py:81
  670.8 4.4 convolution_multiply_fusion.1
  675.2 6.6 scatter_fusion.1
  681.7 48.0 %all-gather.46.cloned.1.call-done = bf16[1,2304,360]{2,1,0:T(8,128)(2,1)} async-done(((bf16[1,144,360]{2,1,0:T(8,128)(2,1)}), bf16[1,2304,360]{2,1,0:T(8,128)(2,1)}) %all-gather.46.cloned.1.call-update) | async-done | bytes 1658896 | tf_op jit(solution)/shard_map/all_gather | solution.py:69
  731.8 56.8 %all-gather.48.cloned.1.call-done = bf16[1,2304,360]{2,1,0:T(8,128)(2,1)} async-done(((bf16[1,144,360]{2,1,0:T(8,128)(2,1)}), bf16[1,2304,360]{2,1,0:T(8,128)(2,1)}) %all-gather.48.cloned.1.call-update) | async-done | bytes 1658896 | tf_op jit(solution)/shard_map/all_gather | solution.py:70
  788.6 59.5 %all-gather.50.cloned.1.call-done = bf16[1,360,2304]{1,2,0:T(8,128)(2,1)} async-done(((bf16[1,360,144]{1,2,0:T(8,128)(2,1)}), bf16[1,360,2304]{1,2,0:T(8,128)(2,1)}) %all-gather.50.cloned.1.call-update) | async-done | bytes 1658896 | tf_op jit(solution)/shard_map/all_gather | solution.py:81
  848.1 4.4 convolution_multiply_fusion
  852.5 6.5 scatter_fusion.2
  864.3 68.9 %reduce-scatter.4.cloned.1.call-done = bf16[144,256]{1,0:T(8,128)(2,1)} async-done(((bf16[2304,256]{1,0:T(8,128)(2,1)}), bf16[144,256]{1,0:T(8,128)(2,1)}) %reduce-scatter.4.cloned.1.call-update) | async-done | bytes 73744
  935.6 32.5 %psum.22 = f32[4]{0:T(128)S(1)} all-reduce(f32[4]{0:T(128)S(1)} %multiply_reduce_fusion.1), channel_id=1, replica_groups=mesh['dp'=16,'mp'=16] {'mp'}, use_global_device_ids=true, to_apply=%region_35.36 | all-reduce | flops 4 | bytes 32 | tf_op jit(solution)/shard_map/psum | solution.py:98
  968.3 610.6 %all_gather.55 = bf16[256,4,144]{2,1,0:T(4,128)(2,1)S(1)} all-gather(bf16[1,4,144]{2,1,0:T(4,128)(2,1)S(1)} %fusion.79), channel_id=1, replica_groups=mesh['dp'=16,'mp'=16] {'dp','mp'}, dimensions={0}, use_global_device_ids=true | all-gather | bytes 296064 | tf_op jit(solution)/shard_map/all_gather | solution.py:105
  1580.2 101.6 %pmax.7 = f32[64]{0:T(128)S(1)} all-reduce(f32[64]{0:T(128)S(1)} %get-tuple-element.38), channel_id=1, replica_groups=mesh['dp'=16,'mp'=16] {'dp','mp'}, use_global_device_ids=true, to_apply=%region_37.38 | all-reduce | flops 64 | bytes 512 | tf_op jit(solution)/shard_map/pmax | solution.py:114
  1682.0 74.5 %psum.23 = f32[64]{0:T(128)S(1)} all-reduce(f32[64]{0:T(128)S(1)} %exponential_reduce_fusion), channel_id=1, replica_groups=mesh['dp'=16,'mp'=16] {'dp','mp'}, use_global_device_ids=true, to_apply=%region_39.40 | all-reduce | flops 64 | bytes 512 | tf_op jit(solution)/shard_map/psum | solution.py:115
  (164 shorter events, 71.2 us)
Async XLA Ops:
  7.2 1572.4 %copy-start = (bf16[2304,512]{1,0:T(8,128)(2,1)S(1)}, bf16[2304,512]{1,0:T(8,128)(2,1)}, u32[]{:S(2)}) copy-start(bf16[2304,512]{1,0:T(8,128)(2,1)} %param.20) | copy-start | bytes 7077892
  7.2 45.2 %copy-start.5 = (bf16[4,360,144]{1,2,0:T(8,128)(2,1)S(1)}, bf16[4,360,144]{1,2,0:T(8,128)(2,1)}, u32[]{:S(2)}) copy-start(bf16[4,360,144]{1,2,0:T(8,128)(2,1)} %param.18) | copy-start | bytes 1244164
  7.2 120.0 %all-gather.26.cloned.1.call-start = ((), (), s32[]{:S(2)}) async-start(), calls=%async_computation.1 | async-start | bytes 1253376 | tf_op jit(solution)/shard_map/all_gather | solution.py:49
  48.5 150.5 %all-gather.28.cloned.1.call-start = ((), (), s32[]{:S(2)}) async-start(), calls=%async_computation.2 | async-start | bytes 1880064 | tf_op jit(solution)/shard_map/all_gather | solution.py:69
  50.3 8.9 copy-start.6
  50.4 76.8 %copy-start.7 = (bf16[2304,4]{0,1:T(4,128)(2,1)S(1)}, bf16[2304,4]{0,1:T(4,128)(2,1)}, u32[]{:S(2)}) copy-start(bf16[2304,4]{0,1:T(4,128)(2,1)} %param.15) | copy-start | bytes 55300
  50.4 207.5 %all-gather.30.cloned.1.call-start = ((), (), s32[]{:S(2)}) async-start(), calls=%async_computation.3 | async-start | bytes 1880064 | tf_op jit(solution)/shard_map/all_gather | solution.py:70
  52.3 264.5 %all-gather.32.cloned.1.call-start = ((), (), s32[]{:S(2)}) async-start(), calls=%async_computation.4 | async-start | bytes 1880064 | tf_op jit(solution)/shard_map/all_gather | solution.py:81
  53.2 322.4 %all-gather.34.cloned.1.call-start = ((), (), s32[]{:S(2)}) async-start(), calls=%async_computation.5 | async-start | bytes 1880064 | tf_op jit(solution)/shard_map/all_gather | solution.py:69
  53.8 380.7 %all-gather.36.cloned.1.call-start = ((), (), s32[]{:S(2)}) async-start(), calls=%async_computation.6 | async-start | bytes 1880064 | tf_op jit(solution)/shard_map/all_gather | solution.py:70
  54.3 439.6 %all-gather.38.cloned.1.call-start = ((), (), s32[]{:S(2)}) async-start(), calls=%async_computation.7 | async-start | bytes 1880064 | tf_op jit(solution)/shard_map/all_gather | solution.py:81
  55.1 497.9 %all-gather.40.cloned.1.call-start = ((), (), s32[]{:S(2)}) async-start(), calls=%async_computation.8 | async-start | bytes 1880064 | tf_op jit(solution)/shard_map/all_gather | solution.py:69
  55.8 556.1 %all-gather.42.cloned.1.call-start = ((), (), s32[]{:S(2)}) async-start(), calls=%async_computation.9 | async-start | bytes 1880064 | tf_op jit(solution)/shard_map/all_gather | solution.py:70
  56.6 614.2 %all-gather.44.cloned.1.call-start = ((), (), s32[]{:S(2)}) async-start(), calls=%async_computation.10 | async-start | bytes 1880064 | tf_op jit(solution)/shard_map/all_gather | solution.py:81
  57.2 672.6 %all-gather.46.cloned.1.call-start = ((), (), s32[]{:S(2)}) async-start(), calls=%async_computation.11 | async-start | bytes 1880064 | tf_op jit(solution)/shard_map/all_gather | solution.py:69
  57.9 730.7 %all-gather.48.cloned.1.call-start = ((), (), s32[]{:S(2)}) async-start(), calls=%async_computation.12 | async-start | bytes 1880064 | tf_op jit(solution)/shard_map/all_gather | solution.py:70
  58.5 789.7 %all-gather.50.cloned.1.call-start = ((), (), s32[]{:S(2)}) async-start(), calls=%async_computation.13 | async-start | bytes 1880064 | tf_op jit(solution)/shard_map/all_gather | solution.py:81
  59.2 873.9 %reduce-scatter.4.cloned.1.call-start = ((), (), s32[]{:S(2)}) async-start(), calls=%async_computation.14 | async-start | bytes 1253376
  71.0 0.6 copy-start.14
  77.7 4.4 copy-start.10
  83.5 43.6 %copy-start.8 = (s32[160]{0:T(256)}, s32[160]{0:T(256)S(1)}, u32[]{:S(2)}) copy-start(s32[160]{0:T(256)S(1)} %get-tuple-element.31) | copy-start | bytes 1924
  152.0 2.2 copy-start.12
  152.0 3.0 copy-start.13
  154.2 162.5 %copy-start.4 = (bf16[160,2304]{1,0:T(8,128)(2,1)S(1)}, bf16[160,2304]{1,0:T(8,128)(2,1)}, u32[]{:S(2)}) copy-start(bf16[160,2304]{1,0:T(8,128)(2,1)} %gather_fusion) | copy-start | bytes 2211844
  321.2 54.4 %copy-start.3 = (bf16[160,2304]{1,0:T(8,128)(2,1)S(1)}, bf16[160,2304]{1,0:T(8,128)(2,1)}, u32[]{:S(2)}) copy-start(bf16[160,2304]{1,0:T(8,128)(2,1)} %gather_fusion.2) | copy-start | bytes 2211844
  498.4 54.6 %copy-start.2 = (bf16[160,2304]{1,0:T(8,128)(2,1)S(1)}, bf16[160,2304]{1,0:T(8,128)(2,1)}, u32[]{:S(2)}) copy-start(bf16[160,2304]{1,0:T(8,128)(2,1)} %gather_fusion.4) | copy-start | bytes 2211844
  555.0 120.2 %copy-start.11 = (s32[160]{0:T(256)S(1)}, s32[160]{0:T(256)}, u32[]{:S(2)}) copy-start(s32[160]{0:T(256)} %copy-done.10) | copy-start | bytes 1924
  675.2 54.6 %copy-start.1 = (bf16[160,2304]{1,0:T(8,128)(2,1)S(1)}, bf16[160,2304]{1,0:T(8,128)(2,1)}, u32[]{:S(2)}) copy-start(bf16[160,2304]{1,0:T(8,128)(2,1)} %gather_fusion.6) | copy-start | bytes 2211844
  731.8 120.7 %copy-start.9 = (s32[160]{0:T(256)S(1)}, s32[160]{0:T(256)}, u32[]{:S(2)}) copy-start(s32[160]{0:T(256)} %copy-done.8) | copy-start | bytes 1924
  860.8 2.5 copy-start.15
  860.8 3.5 copy-start.16
Sparse Core Ops, SparseCore 0:
  48.6 78.5 all-gather.25
  129.8 69.1 all-gather.27
  201.6 56.3 all-gather.29
  260.4 56.3 all-gather.31
  319.2 56.3 all-gather.33
  378.1 56.3 all-gather.35
  437.6 56.3 all-gather.37
  496.6 56.3 all-gather.39
  555.6 56.3 all-gather.41
  614.4 56.3 all-gather.43
  673.4 56.3 all-gather.45
  732.2 56.3 all-gather.47
  791.8 56.3 all-gather.49
  862.3 70.7 reduce-scatter.3
where the time goes:
time: 1770 us; the launch traced here: 1760 us
  blocking collectives  858 us (48%)
  waiting for transfers between devices  769 us (43%)
  local copies, waits for them, and re-layouts  56.7 us (3%)
  other arithmetic  37.7 us (2%)
  matrix products  28 us (2%)
    all_gather x1, blocking collectives, body(): lax.all_gather(end_normed[None], ('dp', 'mp'), axis=0, tiled=True)  611 us
    all_gather x4, waiting for transfers between devices, body(): lax.all_gather(specialist_contract_weights[expert], 'dp', axis=1, tiled=T...  237 us
    all_gather x4, waiting for transfers between devices, body(): lax.all_gather(specialist_expand_weights[expert], 'dp', axis=0, tiled=True)  227 us
    all_gather x4, waiting for transfers between devices, body(): lax.all_gather(specialist_switch_weights[expert], 'dp', axis=0, tiled=True)  187 us
    pmax x1, blocking collectives, body(): largest = lax.pmax(jnp.max(lexicon_logit_values, axis=1), ('dp', 'mp'))  102 us
    unnamed x15, waiting for transfers between devices  74.5 us
    psum x1, blocking collectives, body(): lax.psum(jnp.sum(jnp.exp(lexicon_logit_values - largest[:, None]), axis=1...  74.5 us
    all_gather x1, waiting for transfers between devices, body(): features = lax.all_gather(normed_local, 'mp', axis=1, tiled=True)  43 us
  transfers between devices with their start and end apart: 14, of which 14 were waited for; matrix products, arithmetic and copies ran while one was open for 6% of the time, Pallas kernels for 0%

commit v1 on v0

--- a/solution.py
+++ b/solution.py
@@ -46,7 +46,15 @@
         * lax.rsqrt(squares / EMBED_DIMENSION + epsilon)[:, None]
         * premix_rmsnorm_gain
     ).astype(jnp.bfloat16)
-    features = lax.all_gather(normed_local, "mp", axis=1, tiled=True)
+    features = jnp.concatenate(
+        lax.all_to_all(
+            jnp.stack([normed_local] * lax.axis_size("mp"), 0),
+            axis_name="mp",
+            split_axis=0,
+            concat_axis=0,
+        ),
+        1,
+    )
     router = jnp.dot(features, dispatcher_weights, preferred_element_type=jnp.float32)
     mixing = jax.nn.softmax(jnp.take_along_axis(router, chosen_specialists, axis=1), axis=1)
     tables = [slot_tables(chosen_specialists, expert, CAP) for expert in range(experts)]

time: 1770 us -> 1650 us (0.932)
  waiting for transfers between devices: 769 us -> 622 us
    all_gather x4, waiting for transfers between devices: 227 us -> 171 us  [body(): lax.all_gather(specialist_expand_weights[expert], 'dp', axis=0, tiled=True)]
    all_gather x1 -> x0, waiting for transfers between devices: 43 us -> none  [body(): features = lax.all_gather(normed_local, 'mp', axis=1, tiled=True)]
    all_gather x4, waiting for transfers between devices: 187 us -> 145 us  [body(): lax.all_gather(specialist_switch_weights[expert], 'dp', axis=0, tiled=True)]
    unnamed x15 -> x14, waiting for transfers between devices: 74.5 us -> 75.4 us
  transfers between devices with their start and end apart: 14 -> 14, of which waited for: 14 -> 11; matrix products, arithmetic and copies ran while one was open for 6% -> 7% of each run, Pallas kernels for 0% -> 0%
where the time goes in v1:
time: 1650 us; the launch traced here: 1640 us
  blocking collectives  857 us (52%)
  waiting for transfers between devices  622 us (38%)
  local copies, waits for them, and re-layouts  68.7 us (4%)
  other arithmetic  46.8 us (3%)
  matrix products  27.9 us (2%)
    all_gather x1, blocking collectives, body(): lax.all_gather(end_normed[None], ('dp', 'mp'), axis=0, tiled=True)  610 us
    all_gather x4, waiting for transfers between devices, body(): lax.all_gather(specialist_contract_weights[expert], 'dp', axis=1, tiled=T...  231 us
    all_gather x4, waiting for transfers between devices, body(): lax.all_gather(specialist_expand_weights[expert], 'dp', axis=0, tiled=True)  171 us
    all_gather x4, waiting for transfers between devices, body(): lax.all_gather(specialist_switch_weights[expert], 'dp', axis=0, tiled=True)  145 us
    pmax x1, blocking collectives, body(): largest = lax.pmax(jnp.max(lexicon_logit_values, axis=1), ('dp', 'mp'))  102 us
    unnamed x14, waiting for transfers between devices  75.4 us
    psum x1, blocking collectives, body(): lax.psum(jnp.sum(jnp.exp(lexicon_logit_values - largest[:, None]), axis=1...  74.5 us
    psum x1, blocking collectives, body(): lax.psum(jnp.sum(skip_stream_arriving * skip_stream_arriving, axis=1), 'mp')  38.5 us
  transfers between devices with their start and end apart: 14, of which 11 were waited for; matrix products, arithmetic and copies ran while one was open for 7% of the time, Pallas kernels for 0%

profile of v1, /device:TPU:1, one launch (start us, length us, event | category | flops | bytes accessed | tf_op | source)
XLA Modules:
  0.0 1640.6 jit_solution(15547742844517644709)
XLA Ops:
  17.4 38.5 %psum.21 = f32[256]{0:T(256)S(1)} all-reduce(f32[256]{0:T(256)S(1)} %multiply_reduce_fusion), channel_id=1, replica_groups=mesh['dp'=16,'mp'=16] {'mp'}, use_global_device_ids=true, to_apply=%region_5.6 | all-reduce | flops 256 | bytes 2048 | tf_op jit(solution)/shard_map/psum | solution.py:43
  57.2 3.7 all-to-all-start
  92.5 2.5 scatter_custom_fusion.14
  110.2 4.9 gather_fusion.9
  123.9 2.3 gather_fusion.2
  126.2 2.6 gather_fusion.1
  131.0 2.6 gather_fusion.7
  133.6 2.2 gather_fusion.6
  138.5 2.3 fusion.18
  140.7 53.3 %all-gather.29.cloned.1.call-done = bf16[1,360,2304]{1,2,0:T(8,128)(2,1)} async-done(((bf16[1,360,144]{1,2,0:T(8,128)(2,1)}), bf16[1,360,2304]{1,2,0:T(8,128)(2,1)}) %all-gather.29.cloned.1.call-update) | async-done | bytes 1658896 | tf_op jit(solution)/shard_map/all_gather | solution.py:89
  194.1 4.4 convolution_multiply_fusion.3
  198.5 5.2 scatter_custom_fusion.3
  203.7 49.3 %all-gather.31.cloned.1.call-done = bf16[1,2304,360]{2,1,0:T(8,128)(2,1)} async-done(((bf16[1,144,360]{2,1,0:T(8,128)(2,1)}), bf16[1,2304,360]{2,1,0:T(8,128)(2,1)}) %all-gather.31.cloned.1.call-update) | async-done | bytes 1658896 | tf_op jit(solution)/shard_map/all_gather | solution.py:77
  255.0 56.8 %all-gather.33.cloned.1.call-done = bf16[1,2304,360]{2,1,0:T(8,128)(2,1)} async-done(((bf16[1,144,360]{2,1,0:T(8,128)(2,1)}), bf16[1,2304,360]{2,1,0:T(8,128)(2,1)}) %all-gather.33.cloned.1.call-update) | async-done | bytes 1658896 | tf_op jit(solution)/shard_map/all_gather | solution.py:78
  311.8 58.8 %all-gather.35.cloned.1.call-done = bf16[1,360,2304]{1,2,0:T(8,128)(2,1)} async-done(((bf16[1,360,144]{1,2,0:T(8,128)(2,1)}), bf16[1,360,2304]{1,2,0:T(8,128)(2,1)}) %all-gather.35.cloned.1.call-update) | async-done | bytes 1658896 | tf_op jit(solution)/shard_map/all_gather | solution.py:89
  370.6 4.3 convolution_multiply_fusion.2
  374.9 6.5 scatter_fusion
  381.5 48.1 %all-gather.37.cloned.1.call-done = bf16[1,2304,360]{2,1,0:T(8,128)(2,1)} async-done(((bf16[1,144,360]{2,1,0:T(8,128)(2,1)}), bf16[1,2304,360]{2,1,0:T(8,128)(2,1)}) %all-gather.37.cloned.1.call-update) | async-done | bytes 1658896 | tf_op jit(solution)/shard_map/all_gather | solution.py:77
  431.6 56.9 %all-gather.39.cloned.1.call-done = bf16[1,2304,360]{2,1,0:T(8,128)(2,1)} async-done(((bf16[1,144,360]{2,1,0:T(8,128)(2,1)}), bf16[1,2304,360]{2,1,0:T(8,128)(2,1)}) %all-gather.39.cloned.1.call-update) | async-done | bytes 1658896 | tf_op jit(solution)/shard_map/all_gather | solution.py:78
  488.5 59.0 %all-gather.41.cloned.1.call-done = bf16[1,360,2304]{1,2,0:T(8,128)(2,1)} async-done(((bf16[1,360,144]{1,2,0:T(8,128)(2,1)}), bf16[1,360,2304]{1,2,0:T(8,128)(2,1)}) %all-gather.41.cloned.1.call-update) | async-done | bytes 1658896 | tf_op jit(solution)/shard_map/all_gather | solution.py:89
  547.5 4.4 convolution_multiply_fusion.1
  551.9 6.5 scatter_fusion.1
  558.5 47.9 %all-gather.43.cloned.1.call-done = bf16[1,2304,360]{2,1,0:T(8,128)(2,1)} async-done(((bf16[1,144,360]{2,1,0:T(8,128)(2,1)}), bf16[1,2304,360]{2,1,0:T(8,128)(2,1)}) %all-gather.43.cloned.1.call-update) | async-done | bytes 1658896 | tf_op jit(solution)/shard_map/all_gather | solution.py:77
  608.4 57.0 %all-gather.45.cloned.1.call-done = bf16[1,2304,360]{2,1,0:T(8,128)(2,1)} async-done(((bf16[1,144,360]{2,1,0:T(8,128)(2,1)}), bf16[1,2304,360]{2,1,0:T(8,128)(2,1)}) %all-gather.45.cloned.1.call-update) | async-done | bytes 1658896 | tf_op jit(solution)/shard_map/all_gather | solution.py:78
  665.3 59.4 %all-gather.47.cloned.1.call-done = bf16[1,360,2304]{1,2,0:T(8,128)(2,1)} async-done(((bf16[1,360,144]{1,2,0:T(8,128)(2,1)}), bf16[1,360,2304]{1,2,0:T(8,128)(2,1)}) %all-gather.47.cloned.1.call-update) | async-done | bytes 1658896 | tf_op jit(solution)/shard_map/all_gather | solution.py:89
  724.7 4.4 convolution_multiply_fusion
  729.1 6.5 scatter_fusion.2
  740.9 70.0 %reduce-scatter.4.cloned.1.call-done = bf16[144,256]{1,0:T(8,128)(2,1)} async-done(((bf16[2304,256]{1,0:T(8,128)(2,1)}), bf16[144,256]{1,0:T(8,128)(2,1)}) %reduce-scatter.4.cloned.1.call-update) | async-done | bytes 73744
  813.4 31.6 %psum.22 = f32[4]{0:T(128)S(1)} all-reduce(f32[4]{0:T(128)S(1)} %multiply_reduce_fusion.1), channel_id=1, replica_groups=mesh['dp'=16,'mp'=16] {'mp'}, use_global_device_ids=true, to_apply=%region_35.36 | all-reduce | flops 4 | bytes 32 | tf_op jit(solution)/shard_map/psum | solution.py:106
  845.1 610.4 %all_gather.51 = bf16[256,4,144]{2,1,0:T(4,128)(2,1)S(1)} all-gather(bf16[1,4,144]{2,1,0:T(4,128)(2,1)S(1)} %fusion.79), channel_id=1, replica_groups=mesh['dp'=16,'mp'=16] {'dp','mp'}, dimensions={0}, use_global_device_ids=true | all-gather | bytes 296064 | tf_op jit(solution)/shard_map/all_gather | solution.py:113
  1456.8 101.6 %pmax.7 = f32[64]{0:T(128)S(1)} all-reduce(f32[64]{0:T(128)S(1)} %get-tuple-element.38), channel_id=1, replica_groups=mesh['dp'=16,'mp'=16] {'dp','mp'}, use_global_device_ids=true, to_apply=%region_37.38 | all-reduce | flops 64 | bytes 512 | tf_op jit(solution)/shard_map/pmax | solution.py:122
  1558.6 74.5 %psum.23 = f32[64]{0:T(128)S(1)} all-reduce(f32[64]{0:T(128)S(1)} %exponential_reduce_fusion), channel_id=1, replica_groups=mesh['dp'=16,'mp'=16] {'dp','mp'}, use_global_device_ids=true, to_apply=%region_39.40 | all-reduce | flops 64 | bytes 512 | tf_op jit(solution)/shard_map/psum | solution.py:123
  (182 shorter events, 87.8 us)
Async XLA Ops:
  7.2 1449.0 %copy-start = (bf16[2304,512]{1,0:T(8,128)(2,1)S(1)}, bf16[2304,512]{1,0:T(8,128)(2,1)}, u32[]{:S(2)}) copy-start(bf16[2304,512]{1,0:T(8,128)(2,1)} %param.20) | copy-start | bytes 7077892
  7.2 4.1 copy-start.9
  7.2 10.2 copy-start.8
  7.2 131.3 %all-gather.25.cloned.1.call-start = ((), (), s32[]{:S(2)}) async-start(), calls=%async_computation.2 | async-start | bytes 1880064 | tf_op jit(solution)/shard_map/all_gather | solution.py:77
  9.3 46.7 %copy-start.21 = (f32[144]{0:T(256)S(1)}, f32[144]{0:T(256)}, u32[]{:S(2)}) copy-start(f32[144]{0:T(256)} %param.14) | copy-start | bytes 1732
  9.3 131.5 %all-gather.27.cloned.1.call-start = ((), (), s32[]{:S(2)}) async-start(), calls=%async_computation.3 | async-start | bytes 1880064 | tf_op jit(solution)/shard_map/all_gather | solution.py:78
  11.2 182.9 %all-gather.29.cloned.1.call-start = ((), (), s32[]{:S(2)}) async-start(), calls=%async_computation.4 | async-start | bytes 1880064 | tf_op jit(solution)/shard_map/all_gather | solution.py:89
  12.1 240.8 %all-gather.31.cloned.1.call-start = ((), (), s32[]{:S(2)}) async-start(), calls=%async_computation.5 | async-start | bytes 1880064 | tf_op jit(solution)/shard_map/all_gather | solution.py:77
  12.7 299.1 %all-gather.33.cloned.1.call-start = ((), (), s32[]{:S(2)}) async-start(), calls=%async_computation.6 | async-start | bytes 1880064 | tf_op jit(solution)/shard_map/all_gather | solution.py:78
  13.3 357.3 %all-gather.35.cloned.1.call-start = ((), (), s32[]{:S(2)}) async-start(), calls=%async_computation.7 | async-start | bytes 1880064 | tf_op jit(solution)/shard_map/all_gather | solution.py:89
  13.8 415.7 %all-gather.37.cloned.1.call-start = ((), (), s32[]{:S(2)}) async-start(), calls=%async_computation.8 | async-start | bytes 1880064 | tf_op jit(solution)/shard_map/all_gather | solution.py:77
  14.6 473.9 %all-gather.39.cloned.1.call-start = ((), (), s32[]{:S(2)}) async-start(), calls=%async_computation.9 | async-start | bytes 1880064 | tf_op jit(solution)/shard_map/all_gather | solution.py:78
  15.3 532.2 %all-gather.41.cloned.1.call-start = ((), (), s32[]{:S(2)}) async-start(), calls=%async_computation.10 | async-start | bytes 1880064 | tf_op jit(solution)/shard_map/all_gather | solution.py:89
  16.1 590.3 %all-gather.43.cloned.1.call-start = ((), (), s32[]{:S(2)}) async-start(), calls=%async_computation.11 | async-start | bytes 1880064 | tf_op jit(solution)/shard_map/all_gather | solution.py:77
  16.7 648.7 %all-gather.45.cloned.1.call-start = ((), (), s32[]{:S(2)}) async-start(), calls=%async_computation.12 | async-start | bytes 1880064 | tf_op jit(solution)/shard_map/all_gather | solution.py:78
  56.0 5.5 copy-start.10
  57.2 48.9 %all-to-all-start = ((bf16[16,256,144]{1,2,0:T(8,128)(2,1)}), bf16[16,256,144]{1,2,0:T(8,128)(2,1)S(1)}, u32[]{:S(2)}, u32[]{:S(2)}) async-start(bf16[16,256,144]{1,2,0:T(8,128)(2,1)} %stack.2), calls=%async_computation | async-start | bytes 2359296 | tf_op jit(solution)/shard_map/all_to_all | solution.py:50
  60.9 663.9 %all-gather.47.cloned.1.call-start = ((), (), s32[]{:S(2)}) async-start(), calls=%async_computation.13 | async-start | bytes 1880064 | tf_op jit(solution)/shard_map/all_gather | solution.py:89
  61.5 749.4 %reduce-scatter.4.cloned.1.call-start = ((), (), s32[]{:S(2)}) async-start(), calls=%async_computation.14 | async-start | bytes 1253376
  67.1 4.1 copy-start.22
  76.4 3.8 copy-start.25
  99.4 3.7 copy-start.13
  101.2 3.7 copy-start.15
  133.6 3.6 copy-start.17
  133.6 4.2 copy-start.18
  135.8 58.3 %copy-start.7 = (bf16[160,2304]{1,0:T(8,128)(2,1)S(1)}, bf16[160,2304]{1,0:T(8,128)(2,1)}, u32[]{:S(2)}) copy-start(bf16[160,2304]{1,0:T(8,128)(2,1)} %gather_fusion) | copy-start | bytes 2211844
  198.5 54.4 %copy-start.6 = (bf16[160,2304]{1,0:T(8,128)(2,1)S(1)}, bf16[160,2304]{1,0:T(8,128)(2,1)}, u32[]{:S(2)}) copy-start(bf16[160,2304]{1,0:T(8,128)(2,1)} %gather_fusion.2) | copy-start | bytes 2211844
  255.0 120.0 %copy-start.16 = (s32[160]{0:T(256)S(1)}, s32[160]{0:T(256)}, u32[]{:S(2)}) copy-start(s32[160]{0:T(256)} %copy-done.15) | copy-start | bytes 1924
  374.9 54.6 %copy-start.5 = (bf16[160,2304]{1,0:T(8,128)(2,1)S(1)}, bf16[160,2304]{1,0:T(8,128)(2,1)}, u32[]{:S(2)}) copy-start(bf16[160,2304]{1,0:T(8,128)(2,1)} %gather_fusion.4) | copy-start | bytes 2211844
  431.6 120.3 %copy-start.14 = (s32[160]{0:T(256)S(1)}, s32[160]{0:T(256)}, u32[]{:S(2)}) copy-start(s32[160]{0:T(256)} %copy-done.13) | copy-start | bytes 1924
  551.9 54.5 %copy-start.4 = (bf16[160,2304]{1,0:T(8,128)(2,1)S(1)}, bf16[160,2304]{1,0:T(8,128)(2,1)}, u32[]{:S(2)}) copy-start(bf16[160,2304]{1,0:T(8,128)(2,1)} %gather_fusion.6) | copy-start | bytes 2211844
  608.4 120.8 %copy-start.12 = (s32[160]{0:T(256)S(1)}, s32[160]{0:T(256)}, u32[]{:S(2)}) copy-start(s32[160]{0:T(256)} %copy-done.11) | copy-start | bytes 1924
  (8 other events, 14.6 us)
Sparse Core Ops, SparseCore 0:
  10.7 65.2 all-gather.24
  78.5 56.5 all-gather.26
  137.7 56.3 all-gather.28
  196.6 56.3 all-gather.30
  255.4 56.3 all-gather.32
  314.2 56.3 all-gather.34
  373.2 56.3 all-gather.36
  432.2 56.3 all-gather.38
  491.2 56.3 all-gather.40
  550.0 56.3 all-gather.42
  609.0 56.3 all-gather.44
  668.4 56.3 all-gather.46
  739.0 71.8 reduce-scatter.3
